TPU v7x, 32 devices: a whole 2x2x4 slice. The times are simulated.
32 devices in a mesh: row: 8 (over y, x, core), col: 4 (over z).
Axes of the slice: x: 2, y: 2, z: 4, core: 2. Of those that a mesh axis runs over, the one named last changes fastest.
Arguments:
- tokens: bfloat16 [65536, 1024], P('row', 'col'), may hold values from -6 to 6
- up_weight: bfloat16 [1024, 4096], P('row', 'col'), may hold values from -0.1875 to 0.1875
- hidden_grad: bfloat16 [65536, 4096], P('row', 'col'), may hold values from -6 to 6
Outputs:
- hidden: bfloat16 [65536, 4096], P('row', 'col')
- input_grad: bfloat16 [65536, 1024], P('row', 'col')
All inputs are finite; a program needn't handle non-finite values.
Results may differ from a plain program's by a relative error of at most 0.017.
Values may be sent and summed in bfloat16 or wider, within the bound.
No kernel may reach another device: no remote copies, remote signals or barrier semaphores. Data moves between devices by JAX's collectives and lax.ppermute only.
A program may use at most 128 MiB of HBM per device.

v0:
```python
import jax
import jax.numpy as jnp
from jax import lax
from jax.sharding import PartitionSpec as P

gelu_c = 0.7978845608028654
gelu_a = 0.044715


def gelu_value(v):
    inner = gelu_c * (v + gelu_a * v * v * v)
    return 0.5 * v * (1.0 + jnp.tanh(inner))


def gelu_slope(v):
    inner = gelu_c * (v + gelu_a * v * v * v)
    tval = jnp.tanh(inner)
    return 0.5 * (1.0 + tval) + 0.5 * v * (1.0 - tval * tval) * gelu_c * (
        1.0 + 3.0 * gelu_a * v * v
    )


def per_device(tokens, up_weight, hidden_grad):
    column_panel = lax.all_gather(up_weight, "row", axis=0, tiled=True)
    token_rows = lax.all_gather(tokens, "col", axis=1, tiled=True)
    preact = jnp.dot(token_rows, column_panel, preferred_element_type=jnp.float32)
    hidden = gelu_value(preact).astype(jnp.bfloat16)
    pre_grad = (hidden_grad.astype(jnp.float32) * gelu_slope(preact)).astype(jnp.bfloat16)
    summed = lax.psum_scatter(
        lax.dot_general(
            column_panel, pre_grad, (((1,), (1,)), ((), ())), preferred_element_type=jnp.float32
        ).astype(jnp.bfloat16),
        "col",
        scatter_dimension=0,
        tiled=True,
    ).astype(jnp.float32)
    input_grad = jnp.transpose(summed).astype(jnp.bfloat16)
    return (hidden, input_grad)


def solution(mesh):
    in_specs = (P("row", "col"), P("row", "col"), P("row", "col"))
    out_specs = (P("row", "col"), P("row", "col"))
    return jax.shard_map(
        per_device, mesh=mesh, in_specs=in_specs, out_specs=out_specs, check_vma=False
    )
```

profile of v0, /device:TPU:0, one launch (start us, length us, event | category | flops | bytes accessed | tf_op | source)
XLA Modules:
  0.0 688.1 jit_solution(10581565400900481184)
XLA Ops:
  7.2 0.0 all-gather.5.cloned.1.call-start
  7.2 0.7 all-gather.5.cloned.1.call-update
  7.9 0.0 all-gather.3.cloned.1.call-start
  7.9 0.7 all-gather.3.cloned.1.call-update
  8.6 0.0 reduce-scatter.2.cloned.1.call-start
  8.7 31.7 %all-gather.5.cloned.1.call-done = bf16[1024,1024]{1,0:T(8,128)(2,1)} async-done(((bf16[128,1024]{1,0:T(8,128)(2,1)}), bf16[1024,1024]{1,0:T(8,128)(2,1)}) %all-gather.5.cloned.1.call-update) | async-done | bytes 2097168 | tf_op jit(solution)/shard_map/all_gather | solution.py:24
  40.4 0.0 copy-start
  40.4 287.8 %all-gather.3.cloned.1.call-done = bf16[8192,1024]{1,0:T(8,128)(2,1)} async-done(((bf16[8192,256]{1,0:T(8,128)(2,1)}), bf16[8192,1024]{1,0:T(8,128)(2,1)}) %all-gather.3.cloned.1.call-update) | async-done | bytes 16777232 | tf_op jit(solution)/shard_map/all_gather | solution.py:25
  328.2 34.3 %multiply_convert_fusion = (bf16[8192,1024]{1,0:T(8,128)(2,1)}, f32[8192,1024]{1,0:T(8,128)}) fusion(bf16[8192,1024]{1,0:T(8,128)(2,1)} %all-gather.3.cloned.1.call-done, bf16[1024,1024]{1,0:T(8,128)(2,1)} %all-gather.5.cloned.1.call-done), kind=kOutput, calls=%fused_computation.9 | convolution fusion | flops 17255366656 | bytes 69206016 | tf_op jit(solution)/shard_map/dot_general | solution.py:26
  362.6 0.0 copy-done
  362.6 40.1 %convert_bitcast_fusion = bf16[1024,8192]{0,1:T(8,128)(2,1)} fusion(bf16[1024,1024]{1,0:T(8,128)(2,1)S(1)} %copy-done, f32[8192,1024]{1,0:T(8,128)} %get-tuple-element.3, bf16[8192,1024]{1,0:T(8,128)(2,1)} %param.5), kind=kOutput, calls=%fused_computation.10 | convolution fusion | flops 17356029952 | bytes 69206016 | tf_op jit(solution)/shard_map/dot_general | solution.py:30
  402.7 0.0 reduce-scatter.2.cloned.1.call-update
  402.7 278.8 %reduce-scatter.2.cloned.1.call-done = bf16[256,8192]{0,1:T(8,128)(2,1)} async-done(((bf16[1024,8192]{0,1:T(8,128)(2,1)}), bf16[256,8192]{0,1:T(8,128)(2,1)}) %reduce-scatter.2.cloned.1.call-update) | async-done | bytes 4194320 | tf_op jit(solution)/shard_map/reduce_scatter | solution.py:29
Async XLA Ops:
  7.2 33.2 %all-gather.5.cloned.1.call-start = ((), (), s32[]{:S(2)}) async-start(), calls=%async_computation.2 | async-start | bytes 2359296 | tf_op jit(solution)/shard_map/all_gather | solution.py:24
  7.9 320.3 %all-gather.3.cloned.1.call-start = ((), (), s32[]{:S(2)}) async-start(), calls=%async_computation.1 | async-start | bytes 20971520 | tf_op jit(solution)/shard_map/all_gather | solution.py:25
  8.6 672.9 %reduce-scatter.2.cloned.1.call-start = ((), (), s32[]{:S(2)}) async-start(), calls=%async_computation.3 | async-start | bytes 20971520 | tf_op jit(solution)/shard_map/reduce_scatter | solution.py:29
  40.4 322.2 %copy-start = (bf16[1024,1024]{1,0:T(8,128)(2,1)S(1)}, bf16[1024,1024]{1,0:T(8,128)(2,1)}, u32[]{:S(2)}) copy-start(bf16[1024,1024]{1,0:T(8,128)(2,1)} %all-gather.5.cloned.1.call-done) | copy-start | bytes 6291460
Sparse Core Ops, SparseCore 0:
  9.9 30.4 all-gather.4
  41.9 286.2 all-gather.2
  402.9 278.6 reduce-scatter.1
where the time goes:
time: 688 us
  waiting for transfers between devices  600 us (87%)
  matrix products  74.5 us (11%)
  between operations  13.7 us (2%)
    all_gather x1, waiting for transfers between devices, per_device(): token_rows = lax.all_gather(tokens, 'col', axis=1, tiled=True)  288 us
    reduce_scatter x1, waiting for transfers between devices, per_device(): lax.psum_scatter(lax.dot_general(column_panel, pre_grad, (((1,), (1,)), (...  279 us
    dot_general x1, matrix products, per_device(): lax.dot_general(column_panel, pre_grad, (((1,), (1,)), ((), ())), preferr...  40.1 us
    dot_general x1, matrix products, per_device(): jnp.dot(token_rows, column_panel, preferred_element_type=jnp.float32)  34.3 us
    all_gather x1, waiting for transfers between devices, per_device(): column_panel = lax.all_gather(up_weight, 'row', axis=0, tiled=True)  31.7 us
  transfers between devices with their start and end apart: 3, of which 3 were waited for; matrix products, arithmetic and copies ran while one was open for 0% of the time, Pallas kernels for 0%

commit v1 on v0

--- a/solution.py
+++ b/solution.py
@@ -22,7 +22,12 @@
 
 def per_device(tokens, up_weight, hidden_grad):
     column_panel = lax.all_gather(up_weight, "row", axis=0, tiled=True)
-    token_rows = lax.all_gather(tokens, "col", axis=1, tiled=True)
+    ring = [tokens]
+    for hop in range(3):
+        ring.append(lax.ppermute(ring[-1], "col", [(dev, (dev + 1) % 4) for dev in range(4)]))
+    token_rows = jnp.roll(
+        jnp.concatenate(ring[::-1], axis=1), (lax.axis_index("col") + 1) * ring[0].shape[1], axis=1
+    )
     preact = jnp.dot(token_rows, column_panel, preferred_element_type=jnp.float32)
     hidden = gelu_value(preact).astype(jnp.bfloat16)
     pre_grad = (hidden_grad.astype(jnp.float32) * gelu_slope(preact)).astype(jnp.bfloat16)

time: 688 us -> 684 us (level)
  waiting for transfers between devices: 600 us -> 558 us
  local copies, waits for them, and re-layouts: 0.01 us -> 33.7 us
    all_gather x1 -> x0, waiting for transfers between devices: 288 us -> none  [per_device(): token_rows = lax.all_gather(tokens, 'col', axis=1, tiled=True)]
    ppermute x0 -> x3, waiting for transfers between devices: none -> 279 us  [per_device(): lax.ppermute(ring[-1], 'col', [(dev, (dev + 1) % 4) for dev in range(4)])]
    all_gather x1, waiting for transfers between devices: 31.7 us -> 0.01 us  [per_device(): column_panel = lax.all_gather(up_weight, 'row', axis=0, tiled=True)]
    unnamed x2 -> x15, local copies, waits for them, and re-layouts: 0.01 us -> 31.4 us
  transfers between devices with their start and end apart: 3 -> 5, of which waited for: 3 -> 4; matrix products, arithmetic and copies ran while one was open for 0% -> 5% of each run, Pallas kernels for 0% -> 0%
where the time goes in v1:
time: 684 us; the launch traced here: 683 us
  waiting for transfers between devices  558 us (82%)
  matrix products  74.7 us (11%)
  local copies, waits for them, and re-layouts  33.7 us (5%)
  between operations  14.1 us (2%)
    ppermute x3, waiting for transfers between devices, per_device(): lax.ppermute(ring[-1], 'col', [(dev, (dev + 1) % 4) for dev in range(4)])  279 us
    reduce_scatter x1, waiting for transfers between devices, per_device(): lax.psum_scatter(lax.dot_general(column_panel, pre_grad, (((1,), (1,)), (...  278 us
    dot_general x1, matrix products, per_device(): lax.dot_general(column_panel, pre_grad, (((1,), (1,)), ((), ())), preferr...  40.2 us
    dot_general x1, matrix products, per_device(): jnp.dot(token_rows, column_panel, preferred_element_type=jnp.float32)  34.5 us
    unnamed x15, local copies, waits for them, and re-layouts  31.4 us
  transfers between devices with their start and end apart: 5, of which 4 were waited for; matrix products, arithmetic and copies ran while one was open for 5% of the time, Pallas kernels for 0%

profile of v1, /device:TPU:0, one launch (start us, length us, event | category | flops | bytes accessed | tf_op | source)
XLA Modules:
  0.0 683.3 jit_solution(2086517579136424659)
XLA Ops:
  7.2 0.0 all-gather.2.cloned.1.call-start
  7.2 3.1 collective-permute-start
  10.3 92.8 %collective-permute-done = bf16[8192,256]{1,0:T(8,128)(2,1)S(1)} collective-permute-done((bf16[8192,256]{1,0:T(8,128)(2,1)}, bf16[8192,256]{1,0:T(8,128)(2,1)S(1)}, u32[]{:S(2)}, u32[]{:S(2)}) %collective-permute-start) | collective-permute-done | bytes 4194336 | tf_op jit(solution)/shard_map/ppermute | solution.py:27
  103.1 2.0 copy-done.1
  105.1 0.0 collective-permute-start.1
  105.1 93.6 %collective-permute-done.1 = bf16[8192,256]{1,0:T(8,128)(2,1)} collective-permute-done((bf16[8192,256]{1,0:T(8,128)(2,1)S(1)}, bf16[8192,256]{1,0:T(8,128)(2,1)}, u32[]{:S(2)}, u32[]{:S(2)}) %collective-permute-start.1) | collective-permute-done | bytes 4194336 | tf_op jit(solution)/shard_map/ppermute | solution.py:27
  198.8 0.0 collective-permute-start.2
  198.8 0.0 all-gather.2.cloned.1.call-update
  198.8 0.0 reduce-scatter.2.cloned.1.call-start
  198.9 0.0 copy-start.2
  198.9 0.0 copy-start
  198.9 92.9 %collective-permute-done.2 = bf16[8192,256]{1,0:T(8,128)(2,1)} collective-permute-done((bf16[8192,256]{1,0:T(8,128)(2,1)}, bf16[8192,256]{1,0:T(8,128)(2,1)}, u32[]{:S(2)}, u32[]{:S(2)}) %collective-permute-start.2) | collective-permute-done | bytes 4194336 | tf_op jit(solution)/shard_map/ppermute | solution.py:27
  291.8 4.5 constant_dynamic-update-slice_fusion.7
  296.3 4.5 constant_dynamic-update-slice_fusion.6
  300.8 4.5 constant_dynamic-update-slice_fusion.5
  305.3 4.5 constant_dynamic-update-slice_fusion.4
  309.8 4.5 constant_dynamic-update-slice_fusion.3
  314.3 4.5 constant_dynamic-update-slice_fusion.2
  318.8 2.4 constant_dynamic-update-slice_fusion.1
  321.2 2.3 constant_dynamic-update-slice_fusion
  323.5 34.5 %multiply_convert_fusion = (bf16[8192,1024]{1,0:T(8,128)(2,1)}, f32[8192,1024]{1,0:T(8,128)}) fusion(bf16[1024,1024]{1,0:T(8,128)(2,1)} %all-gather.2.cloned.1.call-done, bf16[8192,2048]{1,0:T(8,128)(2,1)} %constant_dynamic-update-slice_fusion, s32[]{:T(128)S(6)} %select_n.14), kind=kOutput, calls=%fused_computation.9 | convolution fusion | flops 17255366656 | bytes 69206016 | tf_op jit(solution)/shard_map/dot_general | solution.py:31
  358.0 40.2 %convert_bitcast_fusion = bf16[1024,8192]{0,1:T(8,128)(2,1)} fusion(bf16[1024,1024]{1,0:T(8,128)(2,1)S(1)} %copy-done.3, f32[8192,1024]{1,0:T(8,128)} %get-tuple-element.3, bf16[8192,1024]{1,0:T(8,128)(2,1)} %param.5), kind=kOutput, calls=%fused_computation.10 | convolution fusion | flops 17356029952 | bytes 69206016 | tf_op jit(solution)/shard_map/dot_general | solution.py:35
  398.1 0.0 reduce-scatter.2.cloned.1.call-update
  398.2 278.3 %reduce-scatter.2.cloned.1.call-done = bf16[256,8192]{0,1:T(8,128)(2,1)} async-done(((bf16[1024,8192]{0,1:T(8,128)(2,1)}), bf16[256,8192]{0,1:T(8,128)(2,1)}) %reduce-scatter.2.cloned.1.call-update) | async-done | bytes 4194320 | tf_op jit(solution)/shard_map/reduce_scatter | solution.py:34
  (6 shorter events, 0.0 us)
Async XLA Ops:
  7.2 316.3 %all-gather.2.cloned.1.call-start = ((), (), s32[]{:S(2)}) async-start(), calls=%async_computation.1 | async-start | bytes 2359296 | tf_op jit(solution)/shard_map/all_gather | solution.py:24
  7.2 95.9 %collective-permute-start = (bf16[8192,256]{1,0:T(8,128)(2,1)}, bf16[8192,256]{1,0:T(8,128)(2,1)S(1)}, u32[]{:S(2)}, u32[]{:S(2)}) collective-permute-start(bf16[8192,256]{1,0:T(8,128)(2,1)} %param.3), channel_id=1, source_target_pairs={{0,1},{1,2},{2,3},{3,0},{4,5},{5,6},{6,7},{7,4},{8,9},{9,10},{10,1... | collective-permute-start | bytes 12582920 | tf_op jit(solution)/shard_map/ppermute | solution.py:27
  103.1 2.0 copy-start.1
  105.1 93.6 %collective-permute-start.1 = (bf16[8192,256]{1,0:T(8,128)(2,1)S(1)}, bf16[8192,256]{1,0:T(8,128)(2,1)}, u32[]{:S(2)}, u32[]{:S(2)}) collective-permute-start(bf16[8192,256]{1,0:T(8,128)(2,1)S(1)} %collective-permute-done), channel_id=1, source_target_pairs={{0,1},{1,2},{2,3},{3,0},{4,5},{5,6},{6,7},{7,4},{8,9},{9,10},{10,1... | collective-permute-start | bytes 12582920 | tf_op jit(solution)/shard_map/ppermute | solution.py:27
  198.8 93.0 %collective-permute-start.2 = (bf16[8192,256]{1,0:T(8,128)(2,1)}, bf16[8192,256]{1,0:T(8,128)(2,1)}, u32[]{:S(2)}, u32[]{:S(2)}) collective-permute-start(bf16[8192,256]{1,0:T(8,128)(2,1)} %collective-permute-done.1), channel_id=1, source_target_pairs={{0,1},{1,2},{2,3},{3,0},{4,5},{5,6},{6,7},{7,4},{8,9},{9,10},{10,1... | collective-permute-start | bytes 12582920 | tf_op jit(solution)/shard_map/ppermute | solution.py:27
  198.8 477.7 %reduce-scatter.2.cloned.1.call-start = ((), (), s32[]{:S(2)}) async-start(), calls=%async_computation.2 | async-start | bytes 20971520 | tf_op jit(solution)/shard_map/reduce_scatter | solution.py:34
  198.9 119.9 %copy-start.2 = (bf16[8192,256]{1,0:T(8,128)(2,1)S(1)}, bf16[8192,256]{1,0:T(8,128)(2,1)}, u32[]{:S(2)}) copy-start(bf16[8192,256]{1,0:T(8,128)(2,1)} %copy-done.1) | copy-start | bytes 12582916
  198.9 122.3 %copy-start = (bf16[8192,256]{1,0:T(8,128)(2,1)S(1)}, bf16[8192,256]{1,0:T(8,128)(2,1)}, u32[]{:S(2)}) copy-start(bf16[8192,256]{1,0:T(8,128)(2,1)} %param.3) | copy-start | bytes 12582916
  323.5 34.5 %copy-start.3 = (bf16[1024,1024]{1,0:T(8,128)(2,1)S(1)}, bf16[1024,1024]{1,0:T(8,128)(2,1)}, u32[]{:S(2)}) copy-start(bf16[1024,1024]{1,0:T(8,128)(2,1)} %all-gather.2.cloned.1.call-done) | copy-start | bytes 6291460
Sparse Core Ops, SparseCore 0:
  198.9 29.0 all-gather.1
  398.3 278.1 reduce-scatter.1
